TPU v7x, 32 devices: a whole 2x2x4 slice. The times are simulated.
32 devices in a mesh: prow: 8 (over z, core), pcol: 4 (over y, x).
Axes of the slice: x: 2, y: 2, z: 4, core: 2. Of those that a mesh axis runs over, the one named last changes fastest.
Arguments:
- leaf_source: bfloat16 [8, 4, 8, 256, 128], P('prow', 'pcol'), may hold values from -6 to 6
- band_source: bfloat16 [8, 256, 128], P('prow'), may hold values from -6 to 6
- strip_source: bfloat16 [4, 256, 128], P('pcol'), may hold values from -6 to 6
- summit_source: bfloat16 [256, 128], replicated, may hold values from -6 to 6
- leaf_inverse: bfloat16 [8, 4, 8, 256, 256], P('prow', 'pcol'), may hold values from -1 to 2
- band_inverse: bfloat16 [8, 256, 256], P('prow'), may hold values from -1 to 2
- strip_inverse: bfloat16 [4, 256, 256], P('pcol'), may hold values from -1 to 2
- summit_inverse: bfloat16 [256, 256], replicated, may hold values from -1 to 2
- leaf_blocks: bfloat16 [8, 4, 28, 256, 256], P('prow', 'pcol'), may hold values from -0.09375 to 0.09375
- band_blocks: bfloat16 [8, 4, 8, 256, 256], P('prow', 'pcol'), may hold values from -0.046875 to 0.046875
- strip_blocks: bfloat16 [8, 4, 8, 256, 256], P('prow', 'pcol'), may hold values from -0.03125 to 0.03125
- summit_blocks: bfloat16 [8, 4, 8, 256, 256], P('prow', 'pcol'), may hold values from -0.046875 to 0.046875
- coupling: bfloat16 [8, 4, 256, 256], P('prow', 'pcol'), may hold values from -0.09375 to 0.09375
- summit_band: bfloat16 [8, 256, 256], P('prow', 'pcol'), may hold values from -0.078125 to 0.078125
- summit_strip: bfloat16 [4, 256, 256], P('pcol'), may hold values from -0.078125 to 0.078125
- parents: int32 [8, 4, 8], P('prow', 'pcol'), may hold values from 1 to 8, as said below
- widths: int32 [8, 4, 8], P('prow', 'pcol'), may hold values from 64 to 256
Outputs:
- leaf_answer: bfloat16 [8, 4, 8, 256, 128], P('prow', 'pcol')
- band_answer: bfloat16 [8, 256, 128], P('prow')
- strip_answer: bfloat16 [4, 256, 128], P('pcol')
- summit_answer: bfloat16 [256, 128], replicated
Inputs may be any that keep to these rules, and one draw needn't show every extreme that they name: parents[r, c, a] is a later leaf of the same subtree, or 8 where leaf a links only to the separators.
All inputs are finite; a program needn't handle non-finite values.
Results may differ from a plain program's by a relative error of at most 0.015.
Values sent between devices are 32-bit elements; how exact they have to be, the bound alone decides.
No kernel may reach another device: no remote copies, remote signals or barrier semaphores. Data moves between devices by JAX's collectives and lax.ppermute only.
A program may use at most 64 MiB of HBM per device.

v0:
```python
import jax
import jax.numpy as jnp
from jax import lax
from jax.sharding import PartitionSpec as P

PASSES = 2


def ancestors(parent_list, leaf_count):
    node_ids = jnp.arange(leaf_count + 1, dtype=jnp.int32)
    current = parent_list
    extended = jnp.concatenate([current, jnp.full((1,), leaf_count, jnp.int32)])
    reached = jnp.zeros((leaf_count + 1, leaf_count), jnp.float32)
    for repeat in range(leaf_count):
        matches = current[None, :] == node_ids[:, None]
        reached = jnp.maximum(reached, matches.astype(jnp.float32))
        current = jnp.sum(jnp.where(matches, extended[:, None], 0), axis=0)
    return reached[:leaf_count]


def multiply(left, right, form):
    return jnp.einsum(form, left, right, preferred_element_type=jnp.float32)


def forward_block(inverse, source, partial_value):
    residual = (source.astype(jnp.float32) - partial_value).astype(jnp.bfloat16)
    return multiply(inverse, residual, "ij,jr->ir").astype(jnp.bfloat16)


def backward_block(inverse, source, partial_value):
    residual = (source.astype(jnp.float32) - partial_value).astype(jnp.bfloat16)
    return multiply(inverse, residual, "ji,jr->ir").astype(jnp.bfloat16)


def leaf_forward(pair_blocks, inverses, sources, reached, row_mask):
    leaf_count = sources.shape[0]
    solved = []
    for position in range(leaf_count):
        residual = sources[position].astype(jnp.float32)
        if position > 0:
            first_pair = position * (position - 1) // 2
            weights = reached[position, :position].astype(jnp.bfloat16)
            stacked = jnp.stack(solved) * weights[:, None, None]
            residual = residual - multiply(
                pair_blocks[first_pair : first_pair + position], stacked, "bij,bjr->ir"
            )
        residual = (row_mask[position] * residual).astype(jnp.bfloat16)
        solved.append(
            (row_mask[position] * multiply(inverses[position], residual, "ij,jr->ir")).astype(
                jnp.bfloat16
            )
        )
    return jnp.stack(solved)


def leaf_backward(pair_blocks, inverses, solved, outer, reached, row_mask):
    leaf_count = solved.shape[0]
    pending = outer
    answers = [None] * leaf_count
    for position in reversed(range(leaf_count)):
        residual = (
            row_mask[position] * (solved[position].astype(jnp.float32) - pending[position])
        ).astype(jnp.bfloat16)
        update = (row_mask[position] * multiply(inverses[position], residual, "ji,jr->ir")).astype(
            jnp.bfloat16
        )
        answers[position] = update
        if position > 0:
            first_pair = position * (position - 1) // 2
            pushed = multiply(
                pair_blocks[first_pair : first_pair + position], update, "bji,jr->bir"
            )
            pending = pending.at[:position].add(
                reached[position, :position][:, None, None] * pushed
            )
    return jnp.stack(answers)


def per_device(
    leaf_source,
    band_source,
    strip_source,
    summit_source,
    leaf_inverse,
    band_inverse,
    strip_inverse,
    summit_inverse,
    leaf_blocks,
    band_blocks,
    strip_blocks,
    summit_blocks,
    coupling,
    summit_band,
    summit_strip,
    parents,
    widths,
):
    leaf_count = leaf_source.shape[2]
    block_width = leaf_source.shape[3]
    reached = ancestors(parents[0, 0], leaf_count)
    column_ids = jnp.arange(block_width, dtype=jnp.int32)
    row_mask = (column_ids[None, :] < widths[0, 0][:, None]).astype(jnp.float32)[:, :, None]
    band_slab = summit_band.shape[1]
    column_place = lax.axis_index("pcol") * band_slab
    inverses = leaf_inverse[0, 0]
    pair_blocks = leaf_blocks[0, 0]
    to_band = band_blocks[0, 0]
    to_strip = strip_blocks[0, 0]
    to_summit = summit_blocks[0, 0]
    link_block = coupling[0, 0]
    lift_band = summit_band[0]
    lift_strip = summit_strip[0]
    current = (leaf_source[0, 0], band_source[0], strip_source[0], summit_source)
    for iteration in range(PASSES):
        leaf_now, band_now, strip_now, summit_now = current
        solved = leaf_forward(pair_blocks, inverses, leaf_now, reached, row_mask)
        band_term = multiply(to_band, solved, "aij,ajr->ir")
        strip_term = multiply(to_strip, solved, "aij,ajr->ir")
        summit_term = multiply(to_summit, solved, "aij,ajr->ir")
        band_partial = lax.psum(band_term, "pcol")
        band_solved = forward_block(band_inverse[0], band_now, band_partial)
        own_band = lax.dynamic_slice_in_dim(band_solved, column_place, band_slab, 0)
        summit_term = summit_term + multiply(lift_band, own_band, "ki,kn->in")
        strip_term = strip_term + multiply(link_block, band_solved, "ij,jn->in")
        strip_partial, summit_early = lax.psum((strip_term, summit_term), "prow")
        strip_solved = forward_block(strip_inverse[0], strip_now, strip_partial)
        summit_partial = lax.psum(
            summit_early + multiply(lift_strip, strip_solved, "ki,kn->in"), "pcol"
        )
        summit_solved = forward_block(summit_inverse, summit_now, summit_partial)
        summit_answer = backward_block(
            summit_inverse, summit_solved, jnp.zeros(summit_solved.shape, jnp.float32)
        )
        strip_answer = backward_block(
            strip_inverse[0], strip_solved, multiply(lift_strip, summit_answer, "ki,in->kn")
        )
        downward = multiply(link_block, strip_answer, "ji,jn->in")
        band_piece = multiply(lift_band, summit_answer, "ki,in->kn")
        band_back = lax.psum(downward, "pcol") + lax.all_gather(
            band_piece, "pcol", axis=0, tiled=True
        )
        band_answer = backward_block(band_inverse[0], band_solved, band_back)
        outer = (
            multiply(to_band, band_answer, "aij,ir->ajr")
            + multiply(to_strip, strip_answer, "aij,ir->ajr")
            + multiply(to_summit, summit_answer, "aij,ir->ajr")
        )
        leaf_answer = leaf_backward(pair_blocks, inverses, solved, outer, reached, row_mask)
        current = (leaf_answer, band_answer, strip_answer, summit_answer)
    return (current[0][None, None], current[1][None], current[2][None], current[3])


def solution(mesh):
    placed = (
        P("prow", "pcol", None, None, None),
        P("prow", None, None),
        P("pcol", None, None),
        P(),
        P("prow", "pcol", None, None, None),
        P("prow", None, None),
        P("pcol", None, None),
        P(),
        P("prow", "pcol", None, None, None),
        P("prow", "pcol", None, None, None),
        P("prow", "pcol", None, None, None),
        P("prow", "pcol", None, None, None),
        P("prow", "pcol", None, None),
        P("prow", "pcol", None),
        P("pcol", None, None),
        P("prow", "pcol", None),
        P("prow", "pcol", None),
    )
    return jax.shard_map(
        per_device,
        mesh=mesh,
        in_specs=placed,
        out_specs=(
            P("prow", "pcol", None, None, None),
            P("prow", None, None),
            P("pcol", None, None),
            P(),
        ),
        check_vma=False,
    )
```

profile of v0, /device:TPU:0, one launch (start us, length us, event | category | flops | bytes accessed | tf_op | source)
XLA Modules:
  0.0 482.1 jit_solution(6182447190945887679)
XLA Ops:
  17.8 2.1 constant_dynamic-update-slice_fusion.15
  19.8 2.1 constant_dynamic-update-slice_fusion.14
  21.9 2.2 constant_dynamic-update-slice_fusion.13
  25.1 2.5 constant_dynamic-update-slice_fusion.12
  28.4 2.6 constant_dynamic-update-slice_fusion.11
  31.0 2.6 constant_dynamic-update-slice_fusion.18
  33.6 2.2 convolution_bitcast_fusion.21
  40.8 2.1 convolution_bitcast_fusion.19
  43.0 2.1 convolution_bitcast_fusion.20
  45.1 35.8 %all-reduce.11.cloned.1.call-done = f32[256,128]{1,0:T(8,128)} async-done(((f32[256,128]{1,0:T(8,128)}), f32[256,128]{1,0:T(8,128)}) %all-reduce.11.cloned.1.call-update) | async-done | bytes 131088 | tf_op jit(solution)/shard_map/psum | solution.py:120
  87.1 54.4 %all-reduce.25.cloned.1.call-done = (f32[256,128]{1,0:T(8,128)}, f32[256,128]{1,0:T(8,128)}) async-done(((f32[256,128]{1,0:T(8,128)}, f32[256,128]{1,0:T(8,128)}), (f32[256,128]{1,0:T(8,128)}, f32[256,128]{1,0:T(8,128)})) %all-reduce.25.cloned.1.call-update) | async-done | bytes 262160 | tf_op jit(solution)/shard_map/psum | solution.py:125
  146.3 40.2 %all-reduce.13.cloned.1.call-done = f32[256,128]{1,0:T(8,128)} async-done(((f32[256,128]{1,0:T(8,128)}), f32[256,128]{1,0:T(8,128)}) %all-reduce.13.cloned.1.call-update) | async-done | bytes 131088 | tf_op jit(solution)/shard_map/psum | solution.py:127
  186.5 2.0 convolution_convert_fusion.8
  193.0 9.1 %all_gather.6 = f32[256,128]{1,0:T(8,128)} all-gather(f32[64,128]{1,0:T(8,128)S(1)} %convolution_bitcast_fusion.24), channel_id=1, replica_groups=mesh['prow'=8,'pcol'=4] {'pcol'}, dimensions={0}, use_global_device_ids=true | all-gather | bytes 163840 | tf_op jit(solution)/shard_map/all_gather | solution.py:139
  203.8 30.6 %all-reduce.15.cloned.1.call-done = f32[256,128]{0,1:T(8,128)} async-done(((f32[256,128]{0,1:T(8,128)}), f32[256,128]{0,1:T(8,128)}) %all-reduce.15.cloned.1.call-update) | async-done | bytes 131088 | tf_op jit(solution)/shard_map/psum | solution.py:139
  244.6 2.0 constant_dynamic-update-slice_fusion.43
  246.6 2.1 constant_dynamic-update-slice_fusion.42
  248.7 2.2 constant_dynamic-update-slice_fusion.41
  250.9 2.3 constant_dynamic-update-slice_fusion.40
  253.2 2.4 constant_dynamic-update-slice_fusion.39
  255.6 2.5 constant_dynamic-update-slice_fusion.38
  258.1 2.6 constant_dynamic-update-slice_fusion.37
  260.7 2.7 constant_dynamic-update-slice_fusion.44
  263.4 2.2 convolution_bitcast_fusion.15
  265.6 2.2 convolution_bitcast_fusion.17
  267.9 2.2 convolution_bitcast_fusion.16
  270.0 40.1 %all-reduce.17.cloned.1.call-done = f32[256,128]{0,1:T(8,128)} async-done(((f32[256,128]{0,1:T(8,128)}), f32[256,128]{0,1:T(8,128)}) %all-reduce.17.cloned.1.call-update) | async-done | bytes 131088 | tf_op jit(solution)/shard_map/psum | solution.py:120
  315.1 55.6 %all-reduce.23.cloned.1.call-done = (f32[256,128]{0,1:T(8,128)}, f32[256,128]{0,1:T(8,128)}) async-done(((f32[256,128]{0,1:T(8,128)}, f32[256,128]{0,1:T(8,128)}), (f32[256,128]{0,1:T(8,128)}, f32[256,128]{0,1:T(8,128)})) %all-reduce.23.cloned.1.call-update) | async-done | bytes 262160 | tf_op jit(solution)/shard_map/psum | solution.py:125
  374.2 41.4 %all-reduce.19.cloned.1.call-done = f32[256,128]{0,1:T(8,128)} async-done(((f32[256,128]{0,1:T(8,128)}), f32[256,128]{0,1:T(8,128)}) %all-reduce.19.cloned.1.call-update) | async-done | bytes 131088 | tf_op jit(solution)/shard_map/psum | solution.py:127
  415.6 2.0 convolution_convert_fusion.2
  425.4 8.8 %all_gather.7 = f32[256,128]{1,0:T(8,128)S(1)} all-gather(f32[64,128]{1,0:T(8,128)S(1)} %convolution_bitcast_fusion.23), channel_id=1, replica_groups=mesh['prow'=8,'pcol'=4] {'pcol'}, dimensions={0}, use_global_device_ids=true | all-gather | bytes 163840 | tf_op jit(solution)/shard_map/all_gather | solution.py:139
  434.2 29.4 %all-reduce.21.cloned.1.call-done = f32[256,128]{0,1:T(8,128)} async-done(((f32[256,128]{0,1:T(8,128)}), f32[256,128]{0,1:T(8,128)}) %all-reduce.21.cloned.1.call-update) | async-done | bytes 131088 | tf_op jit(solution)/shard_map/psum | solution.py:139
  (273 shorter events, 70.8 us)
Async XLA Ops:
  7.2 26.5 %copy-start = (bf16[1,1,8,256,256]{4,3,2,1,0:T(8,128)(2,1)S(1)}, bf16[1,1,8,256,256]{4,3,2,1,0:T(8,128)(2,1)}, u32[]{:S(2)}) copy-start(bf16[1,1,8,256,256]{4,3,2,1,0:T(8,128)(2,1)} %param.54) | copy-start | bytes 3145732
  7.2 73.7 %all-reduce.11.cloned.1.call-start = ((), (), s32[]{:S(2)}) async-start(), calls=%async_computation | async-start | bytes 262144 | tf_op jit(solution)/shard_map/psum | solution.py:120
  10.5 20.5 %copy-start.73 = (bf16[7]{0:T(256)(128)(2,1)}, bf16[7]{0:T(256)(128)(2,1)S(1)}, u32[]{:S(2)}) copy-start(bf16[7]{0:T(256)(128)(2,1)S(1)} %fusion.586) | copy-start | bytes 46
  10.5 17.8 %copy-start.74 = (bf16[6]{0:T(256)(128)(2,1)}, bf16[6]{0:T(256)(128)(2,1)S(1)}, u32[]{:S(2)}) copy-start(bf16[6]{0:T(256)(128)(2,1)S(1)} %fusion.585) | copy-start | bytes 40
  10.6 14.5 %copy-start.75 = (bf16[5]{0:T(256)(128)(2,1)}, bf16[5]{0:T(256)(128)(2,1)S(1)}, u32[]{:S(2)}) copy-start(bf16[5]{0:T(256)(128)(2,1)S(1)} %fusion.584) | copy-start | bytes 34
  10.6 13.6 %copy-start.76 = (bf16[4]{0:T(256)(128)(2,1)}, bf16[4]{0:T(256)(128)(2,1)S(1)}, u32[]{:S(2)}) copy-start(bf16[4]{0:T(256)(128)(2,1)S(1)} %fusion.583) | copy-start | bytes 28
  10.6 13.5 %copy-start.77 = (bf16[3]{0:T(256)(128)(2,1)}, bf16[3]{0:T(256)(128)(2,1)S(1)}, u32[]{:S(2)}) copy-start(bf16[3]{0:T(256)(128)(2,1)S(1)} %fusion.582) | copy-start | bytes 22
  10.6 13.5 %copy-start.78 = (bf16[2]{0:T(256)(128)(2,1)}, bf16[2]{0:T(256)(128)(2,1)S(1)}, u32[]{:S(2)}) copy-start(bf16[2]{0:T(256)(128)(2,1)S(1)} %fusion.581) | copy-start | bytes 16
  12.0 12.1 %copy-start.55 = (f32[1,256]{1,0:T(1,128)}, f32[1,256]{1,0:T(1,128)S(1)}, u32[]{:S(2)}) copy-start(f32[1,256]{1,0:T(1,128)S(1)} %get-tuple-element.248) | copy-start | bytes 3076
  12.0 13.1 %copy-start.45 = (f32[1,256]{1,0:T(1,128)}, f32[1,256]{1,0:T(1,128)S(1)}, u32[]{:S(2)}) copy-start(f32[1,256]{1,0:T(1,128)S(1)} %get-tuple-element.243) | copy-start | bytes 3076
  12.1 16.3 %copy-start.48 = (f32[1,256]{1,0:T(1,128)}, f32[1,256]{1,0:T(1,128)S(1)}, u32[]{:S(2)}) copy-start(f32[1,256]{1,0:T(1,128)S(1)} %get-tuple-element.242) | copy-start | bytes 3076
  12.1 18.9 %copy-start.51 = (f32[1,256]{1,0:T(1,128)}, f32[1,256]{1,0:T(1,128)S(1)}, u32[]{:S(2)}) copy-start(f32[1,256]{1,0:T(1,128)S(1)} %get-tuple-element.241) | copy-start | bytes 3076
  15.8 11.8 %copy-start.26 = (bf16[128,256]{1,0:T(8,128)(2,1)}, bf16[128,256]{1,0:T(8,128)(2,1)S(1)}, u32[]{:S(2)}) copy-start(bf16[128,256]{1,0:T(8,128)(2,1)S(1)} %get-tuple-element.249) | copy-start | bytes 196612
  17.8 9.8 %copy-start.29 = (bf16[128,256]{1,0:T(8,128)(2,1)}, bf16[128,256]{1,0:T(8,128)(2,1)S(1)}, u32[]{:S(2)}) copy-start(bf16[128,256]{1,0:T(8,128)(2,1)S(1)} %get-tuple-element.250) | copy-start | bytes 196612
  19.8 7.8 %copy-start.31 = (bf16[128,256]{1,0:T(8,128)(2,1)}, bf16[128,256]{1,0:T(8,128)(2,1)S(1)}, u32[]{:S(2)}) copy-start(bf16[128,256]{1,0:T(8,128)(2,1)S(1)} %get-tuple-element.251) | copy-start | bytes 196612
  21.9 5.7 %copy-start.34 = (bf16[128,256]{1,0:T(8,128)(2,1)}, bf16[128,256]{1,0:T(8,128)(2,1)S(1)}, u32[]{:S(2)}) copy-start(bf16[128,256]{1,0:T(8,128)(2,1)S(1)} %get-tuple-element.252) | copy-start | bytes 196612
  25.1 15.7 %copy-start.2 = (bf16[1,1,8,256,256]{4,3,2,1,0:T(8,128)(2,1)S(1)}, bf16[1,1,8,256,256]{4,3,2,1,0:T(8,128)(2,1)}, u32[]{:S(2)}) copy-start(bf16[1,1,8,256,256]{4,3,2,1,0:T(8,128)(2,1)} %param.56) | copy-start | bytes 3145732
  28.4 14.6 %copy-start.1 = (bf16[1,1,8,256,256]{4,3,2,1,0:T(8,128)(2,1)S(1)}, bf16[1,1,8,256,256]{4,3,2,1,0:T(8,128)(2,1)}, u32[]{:S(2)}) copy-start(bf16[1,1,8,256,256]{4,3,2,1,0:T(8,128)(2,1)} %param.55) | copy-start | bytes 3145732
  31.0 51.1 %copy-start.10 = (bf16[1,1,256,256]{3,2,1,0:T(8,128)(2,1)S(1)}, bf16[1,1,256,256]{3,2,1,0:T(8,128)(2,1)}, u32[]{:S(2)}) copy-start(bf16[1,1,256,256]{3,2,1,0:T(8,128)(2,1)} %param.57) | copy-start | bytes 393220
  33.6 107.8 %copy-start.8 = (bf16[1,256,256]{2,1,0:T(8,128)(2,1)S(1)}, bf16[1,256,256]{2,1,0:T(8,128)(2,1)}, u32[]{:S(2)}) copy-start(bf16[1,256,256]{2,1,0:T(8,128)(2,1)} %param.51) | copy-start | bytes 393220
  33.6 109.6 %copy-start.9 = (bf16[1,256,256]{2,1,0:T(8,128)(2,1)S(1)}, bf16[1,256,256]{2,1,0:T(8,128)(2,1)}, u32[]{:S(2)}) copy-start(bf16[1,256,256]{2,1,0:T(8,128)(2,1)} %param.59) | copy-start | bytes 393220
  35.8 105.6 %all-reduce.25.cloned.1.call-start = ((), (), s32[]{:S(2)}) async-start(), calls=%async_computation.7 | async-start | bytes 524288 | tf_op jit(solution)/shard_map/psum | solution.py:125
  85.8 100.7 %all-reduce.13.cloned.1.call-start = ((), (), s32[]{:S(2)}) async-start(), calls=%async_computation.1 | async-start | bytes 262144 | tf_op jit(solution)/shard_map/psum | solution.py:127
  145.0 89.3 %all-reduce.15.cloned.1.call-start = ((), (), s32[]{:S(2)}) async-start(), calls=%async_computation.2 | async-start | bytes 262144 | tf_op jit(solution)/shard_map/psum | solution.py:139
  192.0 118.2 %all-reduce.17.cloned.1.call-start = ((), (), s32[]{:S(2)}) async-start(), calls=%async_computation.3 | async-start | bytes 262144 | tf_op jit(solution)/shard_map/psum | solution.py:120
  234.4 3.6 copy-start.12
  267.8 102.9 %all-reduce.23.cloned.1.call-start = ((), (), s32[]{:S(2)}) async-start(), calls=%async_computation.6 | async-start | bytes 524288 | tf_op jit(solution)/shard_map/psum | solution.py:125
  315.0 100.6 %all-reduce.19.cloned.1.call-start = ((), (), s32[]{:S(2)}) async-start(), calls=%async_computation.4 | async-start | bytes 262144 | tf_op jit(solution)/shard_map/psum | solution.py:127
  374.2 89.4 %all-reduce.21.cloned.1.call-start = ((), (), s32[]{:S(2)}) async-start(), calls=%async_computation.5 | async-start | bytes 262144 | tf_op jit(solution)/shard_map/psum | solution.py:139
  419.5 47.3 %copy-start.13 = (bf16[128,256]{1,0:T(8,128)(2,1)S(1)}, bf16[128,256]{1,0:T(8,128)(2,1)}, u32[]{:S(2)}) copy-start(bf16[128,256]{1,0:T(8,128)(2,1)} %convolution_convert_fusion.1) | copy-start | bytes 196612
  419.5 49.0 %copy-start.11 = (bf16[128,256]{1,0:T(8,128)(2,1)S(1)}, bf16[128,256]{1,0:T(8,128)(2,1)}, u32[]{:S(2)}) copy-start(bf16[128,256]{1,0:T(8,128)(2,1)} %convolution_convert_fusion.2) | copy-start | bytes 196612
  466.1 3.0 copy-start.63
  (55 other events, 89.5 us)
Sparse Core Ops, SparseCore 0:
  36.0 44.9 all-reduce.10
  85.9 55.5 all-reduce.24
  145.1 41.2 all-reduce.12
  192.1 42.2 all-reduce.14
  267.9 42.2 all-reduce.16
  315.1 55.5 all-reduce.22
  374.3 41.2 all-reduce.18
  421.3 42.2 all-reduce.20
where the time goes:
time: 484 us; the launch traced here: 482 us
  waiting for transfers between devices  328 us (68%)
  matrix products  94.3 us (19%)
  local copies, waits for them, and re-layouts  22.6 us (5%)
  blocking collectives  17.8 us (4%)
  between operations  16 us (3%)
    psum x2, waiting for transfers between devices, per_device(): strip_partial, summit_early = lax.psum((strip_term, summit_term), 'prow')  110 us
    dot_general x76, matrix products, multiply(): return jnp.einsum(form, left, right, preferred_element_type=jnp.float32)  94.3 us
    psum x2, waiting for transfers between devices, per_device(): lax.psum(summit_early + multiply(lift_strip, strip_solved, 'ki,kn->in'),...  81.6 us
    psum x2, waiting for transfers between devices, per_device(): band_partial = lax.psum(band_term, 'pcol')  76 us
    psum x2, waiting for transfers between devices, per_device(): lax.psum(downward, 'pcol')  60 us
    all_gather x2, blocking collectives, per_device(): lax.all_gather(band_piece, 'pcol', axis=0, tiled=True)  17.8 us
    unnamed x175, local copies, waits for them, and re-layouts  11.7 us
  transfers between devices with their start and end apart: 8, of which 8 were waited for; matrix products, arithmetic and copies ran while one was open for 4% of the time, Pallas kernels for 0%

commit v1 on v0

--- a/solution.py
+++ b/solution.py
@@ -117,7 +117,11 @@
         band_term = multiply(to_band, solved, "aij,ajr->ir")
         strip_term = multiply(to_strip, solved, "aij,ajr->ir")
         summit_term = multiply(to_summit, solved, "aij,ajr->ir")
-        band_partial = lax.psum(band_term, "pcol")
+        band_partial = band_term
+        for hop in (1, 2):
+            band_partial = band_partial + lax.ppermute(
+                band_partial, "pcol", [(dev, dev ^ hop) for dev in range(4)]
+            )
         band_solved = forward_block(band_inverse[0], band_now, band_partial)
         own_band = lax.dynamic_slice_in_dim(band_solved, column_place, band_slab, 0)
         summit_term = summit_term + multiply(lift_band, own_band, "ki,kn->in")

time: 484 us -> 415 us (0.86)
  waiting for transfers between devices: 328 us -> 259 us
  matrix products: 94.3 us -> 84 us
  starting transfers between devices: 0.33 us -> 7.81 us
    psum x2 -> x0, waiting for transfers between devices: 76 us -> none  [per_device(): band_partial = lax.psum(band_term, 'pcol')]
    dot_general x76, matrix products: 94.3 us -> 84 us  [multiply(): return jnp.einsum(form, left, right, preferred_element_type=jnp.float32)]
    ppermute x0 -> x4, starting transfers between devices: none -> 7.57 us  [per_device(): lax.ppermute(band_partial, 'pcol', [(dev, dev ^ hop) for dev in range(4)])]
    ppermute x0 -> x4, waiting for transfers between devices: none -> 7.01 us  [per_device(): lax.ppermute(band_partial, 'pcol', [(dev, dev ^ hop) for dev in range(4)])]
    unnamed x175 -> x190, local copies, waits for them, and re-layouts: 11.7 us -> 13.2 us
  transfers between devices with their start and end apart: 8 -> 10, of which waited for: 8 -> 9; matrix products, arithmetic and copies ran while one was open for 4% -> 5% of each run, Pallas kernels for 0% -> 0%
where the time goes in v1:
time: 415 us; the launch traced here: 413 us
  waiting for transfers between devices  259 us (62%)
  matrix products  84 us (20%)
  local copies, waits for them, and re-layouts  23.7 us (6%)
  blocking collectives  17.8 us (4%)
  between operations  16 us (4%)
  starting transfers between devices  7.81 us (2%)
  other arithmetic  4.49 us (1%)
    psum x2, waiting for transfers between devices, per_device(): strip_partial, summit_early = lax.psum((strip_term, summit_term), 'prow')  110 us
    dot_general x76, matrix products, multiply(): return jnp.einsum(form, left, right, preferred_element_type=jnp.float32)  84 us
    psum x2, waiting for transfers between devices, per_device(): lax.psum(summit_early + multiply(lift_strip, strip_solved, 'ki,kn->in'),...  81.6 us
    psum x2, waiting for transfers between devices, per_device(): lax.psum(downward, 'pcol')  60 us
    all_gather x2, blocking collectives, per_device(): lax.all_gather(band_piece, 'pcol', axis=0, tiled=True)  17.8 us
    unnamed x190, local copies, waits for them, and re-layouts  13.2 us
  transfers between devices with their start and end apart: 10, of which 9 were waited for; matrix products, arithmetic and copies ran while one was open for 5% of the time, Pallas kernels for 0%

profile of v1, /device:TPU:0, one launch (start us, length us, event | category | flops | bytes accessed | tf_op | source)
XLA Modules:
  0.0 413.0 jit_solution(5174131508977596106)
XLA Ops:
  13.8 1.9 constant_dynamic-update-slice_fusion.17
  15.7 2.0 constant_dynamic-update-slice_fusion.16
  17.7 2.1 constant_dynamic-update-slice_fusion.15
  19.7 2.1 constant_dynamic-update-slice_fusion.14
  21.8 2.2 constant_dynamic-update-slice_fusion.13
  25.0 2.5 constant_dynamic-update-slice_fusion.12
  28.3 2.6 constant_dynamic-update-slice_fusion.11
  30.9 2.6 constant_dynamic-update-slice_fusion.18
  33.5 2.2 convolution_bitcast_fusion.21
  35.7 3.0 collective-permute-start
  50.6 2.0 collective-permute-done.1
  55.8 54.7 %all-reduce.19.cloned.1.call-done = (f32[256,128]{1,0:T(8,128)}, f32[256,128]{1,0:T(8,128)}) async-done(((f32[256,128]{1,0:T(8,128)}, f32[256,128]{1,0:T(8,128)}), (f32[256,128]{1,0:T(8,128)}, f32[256,128]{1,0:T(8,128)})) %all-reduce.19.cloned.1.call-update) | async-done | bytes 262160 | tf_op jit(solution)/shard_map/psum | solution.py:129
  115.3 40.2 %all-reduce.9.cloned.1.call-done = f32[256,128]{1,0:T(8,128)} async-done(((f32[256,128]{1,0:T(8,128)}), f32[256,128]{1,0:T(8,128)}) %all-reduce.9.cloned.1.call-update) | async-done | bytes 131088 | tf_op jit(solution)/shard_map/psum | solution.py:131
  155.5 2.0 convolution_convert_fusion.8
  162.1 9.1 %all_gather.6 = f32[256,128]{1,0:T(8,128)} all-gather(f32[64,128]{1,0:T(8,128)S(1)} %convolution_bitcast_fusion.24), channel_id=1, replica_groups=mesh['prow'=8,'pcol'=4] {'pcol'}, dimensions={0}, use_global_device_ids=true | all-gather | bytes 163840 | tf_op jit(solution)/shard_map/all_gather | solution.py:143
  172.8 30.6 %all-reduce.11.cloned.1.call-done = f32[256,128]{0,1:T(8,128)} async-done(((f32[256,128]{0,1:T(8,128)}), f32[256,128]{0,1:T(8,128)}) %all-reduce.11.cloned.1.call-update) | async-done | bytes 131088 | tf_op jit(solution)/shard_map/psum | solution.py:143
  213.5 2.0 constant_dynamic-update-slice_fusion.43
  215.5 2.1 constant_dynamic-update-slice_fusion.42
  217.6 2.2 constant_dynamic-update-slice_fusion.41
  219.8 2.3 constant_dynamic-update-slice_fusion.40
  222.2 2.4 constant_dynamic-update-slice_fusion.39
  224.5 2.5 constant_dynamic-update-slice_fusion.38
  227.0 2.6 constant_dynamic-update-slice_fusion.37
  229.7 2.7 constant_dynamic-update-slice_fusion.44
  237.0 2.0 collective-permute-done.2
  241.0 3.1 collective-permute-done.3
  246.1 55.6 %all-reduce.17.cloned.1.call-done = (f32[256,128]{0,1:T(8,128)}, f32[256,128]{0,1:T(8,128)}) async-done(((f32[256,128]{0,1:T(8,128)}, f32[256,128]{0,1:T(8,128)}), (f32[256,128]{0,1:T(8,128)}, f32[256,128]{0,1:T(8,128)})) %all-reduce.17.cloned.1.call-update) | async-done | bytes 262160 | tf_op jit(solution)/shard_map/psum | solution.py:129
  305.2 41.4 %all-reduce.13.cloned.1.call-done = f32[256,128]{0,1:T(8,128)} async-done(((f32[256,128]{0,1:T(8,128)}), f32[256,128]{0,1:T(8,128)}) %all-reduce.13.cloned.1.call-update) | async-done | bytes 131088 | tf_op jit(solution)/shard_map/psum | solution.py:131
  346.6 2.0 convolution_convert_fusion.2
  356.4 8.8 %all_gather.7 = f32[256,128]{1,0:T(8,128)S(1)} all-gather(f32[64,128]{1,0:T(8,128)S(1)} %convolution_bitcast_fusion.23), channel_id=1, replica_groups=mesh['prow'=8,'pcol'=4] {'pcol'}, dimensions={0}, use_global_device_ids=true | all-gather | bytes 163840 | tf_op jit(solution)/shard_map/all_gather | solution.py:143
  365.2 29.4 %all-reduce.15.cloned.1.call-done = f32[256,128]{0,1:T(8,128)} async-done(((f32[256,128]{0,1:T(8,128)}), f32[256,128]{0,1:T(8,128)}) %all-reduce.15.cloned.1.call-update) | async-done | bytes 131088 | tf_op jit(solution)/shard_map/psum | solution.py:143
  403.2 1.8 fusion.123
  (292 shorter events, 72.5 us)
Async XLA Ops:
  7.2 26.3 %copy-start = (bf16[1,1,8,256,256]{4,3,2,1,0:T(8,128)(2,1)S(1)}, bf16[1,1,8,256,256]{4,3,2,1,0:T(8,128)(2,1)}, u32[]{:S(2)}) copy-start(bf16[1,1,8,256,256]{4,3,2,1,0:T(8,128)(2,1)} %param.54) | copy-start | bytes 3145732
  7.2 103.4 %all-reduce.19.cloned.1.call-start = ((), (), s32[]{:S(2)}) async-start(), calls=%async_computation.5 | async-start | bytes 524288 | tf_op jit(solution)/shard_map/psum | solution.py:129
  10.5 20.4 %copy-start.80 = (bf16[7]{0:T(256)(128)(2,1)}, bf16[7]{0:T(256)(128)(2,1)S(1)}, u32[]{:S(2)}) copy-start(bf16[7]{0:T(256)(128)(2,1)S(1)} %fusion.586) | copy-start | bytes 46
  10.5 17.7 %copy-start.81 = (bf16[6]{0:T(256)(128)(2,1)}, bf16[6]{0:T(256)(128)(2,1)S(1)}, u32[]{:S(2)}) copy-start(bf16[6]{0:T(256)(128)(2,1)S(1)} %fusion.585) | copy-start | bytes 40
  10.5 14.4 %copy-start.82 = (bf16[5]{0:T(256)(128)(2,1)}, bf16[5]{0:T(256)(128)(2,1)S(1)}, u32[]{:S(2)}) copy-start(bf16[5]{0:T(256)(128)(2,1)S(1)} %fusion.584) | copy-start | bytes 34
  10.6 13.5 %copy-start.83 = (bf16[4]{0:T(256)(128)(2,1)}, bf16[4]{0:T(256)(128)(2,1)S(1)}, u32[]{:S(2)}) copy-start(bf16[4]{0:T(256)(128)(2,1)S(1)} %fusion.583) | copy-start | bytes 28
  10.6 13.5 %copy-start.84 = (bf16[3]{0:T(256)(128)(2,1)}, bf16[3]{0:T(256)(128)(2,1)S(1)}, u32[]{:S(2)}) copy-start(bf16[3]{0:T(256)(128)(2,1)S(1)} %fusion.582) | copy-start | bytes 22
  10.6 13.5 %copy-start.85 = (bf16[2]{0:T(256)(128)(2,1)}, bf16[2]{0:T(256)(128)(2,1)S(1)}, u32[]{:S(2)}) copy-start(bf16[2]{0:T(256)(128)(2,1)S(1)} %fusion.581) | copy-start | bytes 16
  11.9 12.1 %copy-start.62 = (f32[1,256]{1,0:T(1,128)}, f32[1,256]{1,0:T(1,128)S(1)}, u32[]{:S(2)}) copy-start(f32[1,256]{1,0:T(1,128)S(1)} %get-tuple-element.248) | copy-start | bytes 3076
  11.9 13.0 %copy-start.52 = (f32[1,256]{1,0:T(1,128)}, f32[1,256]{1,0:T(1,128)S(1)}, u32[]{:S(2)}) copy-start(f32[1,256]{1,0:T(1,128)S(1)} %get-tuple-element.243) | copy-start | bytes 3076
  12.0 16.3 %copy-start.55 = (f32[1,256]{1,0:T(1,128)}, f32[1,256]{1,0:T(1,128)S(1)}, u32[]{:S(2)}) copy-start(f32[1,256]{1,0:T(1,128)S(1)} %get-tuple-element.242) | copy-start | bytes 3076
  12.0 18.9 %copy-start.58 = (f32[1,256]{1,0:T(1,128)}, f32[1,256]{1,0:T(1,128)S(1)}, u32[]{:S(2)}) copy-start(f32[1,256]{1,0:T(1,128)S(1)} %get-tuple-element.241) | copy-start | bytes 3076
  15.7 11.8 %copy-start.33 = (bf16[128,256]{1,0:T(8,128)(2,1)}, bf16[128,256]{1,0:T(8,128)(2,1)S(1)}, u32[]{:S(2)}) copy-start(bf16[128,256]{1,0:T(8,128)(2,1)S(1)} %get-tuple-element.249) | copy-start | bytes 196612
  25.0 20.0 %copy-start.2 = (bf16[1,1,8,256,256]{4,3,2,1,0:T(8,128)(2,1)S(1)}, bf16[1,1,8,256,256]{4,3,2,1,0:T(8,128)(2,1)}, u32[]{:S(2)}) copy-start(bf16[1,1,8,256,256]{4,3,2,1,0:T(8,128)(2,1)} %param.56) | copy-start | bytes 3145732
  28.3 20.8 %copy-start.1 = (bf16[1,1,8,256,256]{4,3,2,1,0:T(8,128)(2,1)S(1)}, bf16[1,1,8,256,256]{4,3,2,1,0:T(8,128)(2,1)}, u32[]{:S(2)}) copy-start(bf16[1,1,8,256,256]{4,3,2,1,0:T(8,128)(2,1)} %param.55) | copy-start | bytes 3145732
  30.9 21.9 %copy-start.11 = (bf16[1,1,256,256]{3,2,1,0:T(8,128)(2,1)S(1)}, bf16[1,1,256,256]{3,2,1,0:T(8,128)(2,1)}, u32[]{:S(2)}) copy-start(bf16[1,1,256,256]{3,2,1,0:T(8,128)(2,1)} %param.57) | copy-start | bytes 393220
  33.5 77.1 %copy-start.9 = (bf16[1,256,256]{2,1,0:T(8,128)(2,1)S(1)}, bf16[1,256,256]{2,1,0:T(8,128)(2,1)}, u32[]{:S(2)}) copy-start(bf16[1,256,256]{2,1,0:T(8,128)(2,1)} %param.51) | copy-start | bytes 393220
  33.5 78.8 %copy-start.10 = (bf16[1,256,256]{2,1,0:T(8,128)(2,1)S(1)}, bf16[1,256,256]{2,1,0:T(8,128)(2,1)}, u32[]{:S(2)}) copy-start(bf16[1,256,256]{2,1,0:T(8,128)(2,1)} %param.59) | copy-start | bytes 393220
  35.7 10.8 %collective-permute-start = (f32[256,128]{0,1:T(8,128)}, f32[256,128]{0,1:T(8,128)}, u32[]{:S(2)}, u32[]{:S(2)}) collective-permute-start(f32[256,128]{0,1:T(8,128)} %convolution_bitcast_fusion.21), channel_id=1, source_target_pairs={{0,1},{1,0},{2,3},{3,2},{4,5},{5,4},{6,7},{7,6},{8,9},{9,8},{10,11... | collective-permute-start | bytes 393224 | tf_op jit(solution)/shard_map/ppermute | solution.py:122
  47.5 5.0 %collective-permute-start.1 = (f32[256,128]{0,1:T(8,128)S(1)}, f32[256,128]{0,1:T(8,128)S(1)}, u32[]{:S(2)}, u32[]{:S(2)}) collective-permute-start(f32[256,128]{0,1:T(8,128)S(1)} %add.186), channel_id=1, source_target_pairs={{0,2},{1,3},{2,0},{3,1},{4,6},{5,7},{6,4},{7,5},{8,10},{9,11},{10,... | collective-permute-start | bytes 393224 | tf_op jit(solution)/shard_map/ppermute | solution.py:122
  54.6 101.0 %all-reduce.9.cloned.1.call-start = ((), (), s32[]{:S(2)}) async-start(), calls=%async_computation | async-start | bytes 262144 | tf_op jit(solution)/shard_map/psum | solution.py:131
  114.1 89.3 %all-reduce.11.cloned.1.call-start = ((), (), s32[]{:S(2)}) async-start(), calls=%async_computation.1 | async-start | bytes 262144 | tf_op jit(solution)/shard_map/psum | solution.py:143
  161.0 140.7 %all-reduce.17.cloned.1.call-start = ((), (), s32[]{:S(2)}) async-start(), calls=%async_computation.4 | async-start | bytes 524288 | tf_op jit(solution)/shard_map/psum | solution.py:129
  232.3 11.7 %copy-start.13 = (bf16[1,256,256]{2,1,0:T(8,128)(2,1)S(1)}, bf16[1,256,256]{2,1,0:T(8,128)(2,1)}, u32[]{:S(2)}) copy-start(bf16[1,256,256]{2,1,0:T(8,128)(2,1)} %param.50) | copy-start | bytes 393220
  232.3 11.7 %copy-start.22 = (bf16[128,256]{1,0:T(8,128)(2,1)S(1)}, bf16[128,256]{1,0:T(8,128)(2,1)}, u32[]{:S(2)}) copy-start(bf16[128,256]{1,0:T(8,128)(2,1)} %copy-done.21) | copy-start | bytes 196612
  232.3 11.9 %copy-start.24 = (bf16[1,64,256]{2,1,0:T(8,128)(2,1)S(1)}, bf16[1,64,256]{2,1,0:T(8,128)(2,1)}, u32[]{:S(2)}) copy-start(bf16[1,64,256]{2,1,0:T(8,128)(2,1)} %param.58) | copy-start | bytes 98308
  234.0 5.0 %collective-permute-start.2 = (f32[256,128]{0,1:T(8,128)S(1)}, f32[256,128]{0,1:T(8,128)S(1)}, u32[]{:S(2)}, u32[]{:S(2)}) collective-permute-start(f32[256,128]{0,1:T(8,128)S(1)} %convolution_bitcast_fusion.17), channel_id=1, source_target_pairs={{0,1},{1,0},{2,3},{3,2},{4,5},{5,4},{6,7},{7,6},{8,9},{9,8},{10,11... | collective-permute-start | bytes 393224 | tf_op jit(solution)/shard_map/ppermute | solution.py:122
  239.0 5.0 %collective-permute-start.3 = (f32[256,128]{0,1:T(8,128)S(1)}, f32[256,128]{0,1:T(8,128)S(1)}, u32[]{:S(2)}, u32[]{:S(2)}) collective-permute-start(f32[256,128]{0,1:T(8,128)S(1)} %add.205), channel_id=1, source_target_pairs={{0,2},{1,3},{2,0},{3,1},{4,6},{5,7},{6,4},{7,5},{8,10},{9,11},{10,... | collective-permute-start | bytes 393224 | tf_op jit(solution)/shard_map/ppermute | solution.py:122
  246.0 100.6 %all-reduce.13.cloned.1.call-start = ((), (), s32[]{:S(2)}) async-start(), calls=%async_computation.2 | async-start | bytes 262144 | tf_op jit(solution)/shard_map/psum | solution.py:131
  305.2 89.4 %all-reduce.15.cloned.1.call-start = ((), (), s32[]{:S(2)}) async-start(), calls=%async_computation.3 | async-start | bytes 262144 | tf_op jit(solution)/shard_map/psum | solution.py:143
  350.5 47.3 %copy-start.16 = (bf16[128,256]{1,0:T(8,128)(2,1)S(1)}, bf16[128,256]{1,0:T(8,128)(2,1)}, u32[]{:S(2)}) copy-start(bf16[128,256]{1,0:T(8,128)(2,1)} %convolution_convert_fusion.1) | copy-start | bytes 196612
  350.5 49.0 %copy-start.14 = (bf16[128,256]{1,0:T(8,128)(2,1)S(1)}, bf16[128,256]{1,0:T(8,128)(2,1)}, u32[]{:S(2)}) copy-start(bf16[128,256]{1,0:T(8,128)(2,1)} %convolution_convert_fusion.2) | copy-start | bytes 196612
  (64 other events, 148.9 us)
Sparse Core Ops, SparseCore 0:
  54.7 55.8 all-reduce.18
  114.2 41.2 all-reduce.8
  161.2 42.2 all-reduce.10
  246.1 55.5 all-reduce.16
  305.3 41.2 all-reduce.12
  352.3 42.2 all-reduce.14
